TPU v7x, 32 devices: a whole 2x2x4 slice. The times are simulated.
32 devices in a mesh: ctx: 4 (over z), node: 4 (over y, core), local: 2 (over x).
Axes of the slice: x: 2, y: 2, z: 4, core: 2. Of those that a mesh axis runs over, the one named last changes fastest.
Arguments:
- tokens: bfloat16 [1024, 3584], P(('node', 'local'), 'ctx'), may hold values from -6 to 6
- expert_ids: int32 [1024, 4], P(('node', 'local')), may hold values from 0 to 7, as said below
- route_scores: float32 [1024, 4], P(('node', 'local')), may hold values from 0.05 to 1
- w_gate: bfloat16 [8, 3584, 2048], P(('node', 'local'), None, 'ctx'), may hold values from -0.09375 to 0.09375
- w_up: bfloat16 [8, 3584, 2048], P(('node', 'local'), None, 'ctx'), may hold values from -0.09375 to 0.09375
- w_down: bfloat16 [8, 2048, 3584], P(('node', 'local'), None, 'ctx'), may hold values from -0.125 to 0.125
- shared_gate: bfloat16 [3584, 2048], P(None, 'ctx'), may hold values from -0.09375 to 0.09375
- shared_up: bfloat16 [3584, 2048], P(None, 'ctx'), may hold values from -0.09375 to 0.09375
- shared_down: bfloat16 [2048, 3584], P(None, 'ctx'), may hold values from -0.125 to 0.125
Outputs:
- mixed: bfloat16 [1024, 3584], P(('node', 'local'), 'ctx')
Inputs may be any that keep to these rules, and one draw needn't show every extreme that they name: `expert_ids`: each row names 4 different experts: two in each of two different node groups, where expert e lies in group e // 2. In each aligned block of 128 rows (the rows of one index of node+local) no group is named by more than 80 rows and no expert more than 80 times; one group, the same in every block, is named by exactly 80 rows in every block, and one of its experts, the same in every block, exactly 80 times.
All inputs are finite; a program needn't handle non-finite values.
Results may differ from a plain program's by a relative error of at most 0.0064.
Values may be sent and summed in bfloat16 or wider, within the bound.
A program may use at most 64 MiB of HBM per device.

v0:
```python
import jax
import jax.numpy as jnp
from jax import lax
from jax.sharding import PartitionSpec as P

route_scale = 2.5


def matmul(left_side, right_side):
    return jnp.dot(left_side, right_side, preferred_element_type=jnp.float32)


def local(
    tokens, expert_ids, route_scores, w_gate, w_up, w_down, shared_gate, shared_up, shared_down
):
    tok_count = tokens.shape[0]
    feat_local = tokens.shape[1]
    top_count = expert_ids.shape[1]
    group_count = lax.axis_size("node")
    member_count = lax.axis_size("local")
    expert_count = group_count * member_count
    group_cap = (10 * tok_count + 4 * group_count - 1) // (4 * group_count)
    capacity = (2 * group_cap + member_count - 1) // member_count
    slot_total = expert_count * capacity
    gate_local = w_gate[0]
    up_local = w_up[0]
    down_local = w_down[0]
    out_width = down_local.shape[1]
    scaled = route_scale * route_scores / jnp.sum(route_scores, axis=1, keepdims=True)
    gate_weights = lax.optimization_barrier(scaled.astype(jnp.bfloat16)).astype(jnp.float32)
    group_range = jnp.arange(group_count, dtype=jnp.int32)
    group_onehot = (expert_ids // member_count)[:, :, None] == group_range[None, None, :]
    flat_ids = expert_ids.reshape(-1)
    pair_count = flat_ids.shape[0]
    onehot = (flat_ids[:, None] == jnp.arange(expert_count, dtype=jnp.int32)[None, :]).astype(
        jnp.int32
    )
    earlier = jnp.cumsum(onehot, axis=0) - onehot
    ranking = jnp.sum(earlier * onehot, axis=1)
    pair_slot = flat_ids * capacity + ranking
    pair_token = jnp.arange(pair_count, dtype=jnp.int32) // top_count
    matches = pair_slot[None, :] == jnp.arange(slot_total, dtype=jnp.int32)[:, None]
    slot_token = jnp.where(
        jnp.any(matches, axis=1),
        jnp.sum(jnp.where(matches, pair_token[None, :], 0), axis=1),
        tok_count,
    )
    padded_tokens = jnp.concatenate([tokens, jnp.zeros((1, feat_local), tokens.dtype)], axis=0)
    send_rows = padded_tokens[slot_token].reshape(group_count, member_count, capacity * feat_local)
    arrived = lax.all_to_all(
        lax.all_to_all(send_rows, "node", split_axis=0, concat_axis=0, tiled=True),
        "local",
        split_axis=1,
        concat_axis=1,
        tiled=True,
    )
    routed_rows = arrived.reshape(slot_total, feat_local)
    stacked = jnp.concatenate([routed_rows, tokens], axis=0)
    segment = lax.all_gather(stacked, "ctx", axis=1, tiled=True)
    routed_part = segment[:slot_total]
    shared_part = segment[slot_total:]
    gate_routed = matmul(routed_part, gate_local)
    up_routed = matmul(routed_part, up_local)
    gate_shared = matmul(shared_part, shared_gate)
    up_shared = matmul(shared_part, shared_up)
    routed_hidden = (jax.nn.silu(gate_routed) * up_routed).astype(jnp.bfloat16)
    shared_hidden = (jax.nn.silu(gate_shared) * up_shared).astype(jnp.bfloat16)
    hidden_stack = jnp.concatenate([routed_hidden, shared_hidden], axis=0)
    segment = lax.all_gather(hidden_stack, "ctx", axis=1, tiled=True)
    routed_out = matmul(segment[:slot_total], down_local)
    shared_out = matmul(segment[slot_total:], shared_down)
    routed_bf = routed_out.astype(jnp.bfloat16)
    sendback = routed_bf.reshape(group_count, member_count, capacity * out_width)
    returned = lax.all_to_all(
        lax.all_to_all(sendback, "node", split_axis=0, concat_axis=0, tiled=True),
        "local",
        split_axis=1,
        concat_axis=1,
        tiled=True,
    )
    returned = returned.reshape(slot_total, out_width)
    pair_out = returned[pair_slot].reshape(tok_count, top_count, out_width).astype(jnp.float32)
    weighted = gate_weights[:, :, None] * pair_out
    group_sum = jnp.einsum(
        "tkg,tkd->tgd", group_onehot.astype(jnp.float32), weighted, precision=lax.Precision.HIGHEST
    )
    rounded = lax.optimization_barrier(group_sum.astype(jnp.bfloat16)).astype(jnp.float32)
    routed_sum = jnp.sum(rounded, axis=1)
    mixed = shared_out + routed_sum
    return mixed.astype(jnp.bfloat16)


def solution(mesh):
    return jax.shard_map(
        local,
        mesh=mesh,
        in_specs=(
            P(("node", "local"), "ctx"),
            P(("node", "local"), None),
            P(("node", "local"), None),
            P(("node", "local"), None, "ctx"),
            P(("node", "local"), None, "ctx"),
            P(("node", "local"), None, "ctx"),
            P(None, "ctx"),
            P(None, "ctx"),
            P(None, "ctx"),
        ),
        out_specs=P(("node", "local"), "ctx"),
        check_vma=False,
    )
```

profile of v0, /device:TPU:0, one launch (start us, length us, event | category | flops | bytes accessed | tf_op | source)
XLA Modules:
  0.0 292.3 jit_solution(5308196414685565889)
XLA Ops:
  6.5 0.0 all-gather.3.cloned.1.call-start
  6.5 0.8 copy.43
  7.3 0.1 eq.52
  7.4 0.1 reshape.109
  7.6 1.1 reduce-window.6
  8.7 0.2 slice_reduce_fusion
  9.0 0.1 fusion.39
  9.1 0.2 fusion.29
  9.3 0.2 select_reduce_fusion
  9.5 1.0 concatenate.9
  10.5 3.1 %gather_fusion = bf16[640,896]{1,0:T(8,128)(2,1)S(1)} fusion(bf16[129,896]{1,0:T(8,128)(2,1)S(1)} %concatenate.9, s32[1024]{0:T(1024)S(1)} %pad_clamp_fusion.1), kind=kCustom, calls=%fused_computation | custom fusion | bytes 2296320 | tf_op jit(solution)/shard_map/gather | solution.py:49
  13.6 0.4 reshape.111
  14.0 19.6 %all_to_all.20 = bf16[4,2,71680]{2,1,0:T(2,128)(2,1)S(1)} all-to-all(bf16[4,2,71680]{2,1,0:T(2,128)(2,1)S(1)} %reshape.111), channel_id=1, replica_groups=mesh['ctx'=4,'node'=4,'local'=2] {'node'}, dimensions={0} | all-to-all | bytes 2293760 | tf_op jit(solution)/shard_map/all_to_all | solution.py:51
  33.5 0.6 copy.45
  34.1 17.1 %all_to_all.21 = bf16[4,2,71680]{2,0,1:T(4,128)(2,1)S(1)} all-to-all(bf16[4,2,71680]{2,0,1:T(4,128)(2,1)S(1)} %copy.45), channel_id=1, replica_groups=mesh['ctx'=4,'node'=4,'local'=2] {'local'}, dimensions={1} | all-to-all | bytes 2293760 | tf_op jit(solution)/shard_map/all_to_all | solution.py:50
  51.3 0.0 copy-start.2
  51.3 1.2 copy.46
  52.4 0.8 reshape.112
  53.2 0.0 copy-done.2
  53.3 1.2 pad_maximum_fusion
  54.5 0.0 all-gather.3.cloned.1.call-update
  54.5 0.0 all-gather.5.cloned.1.call-start
  54.6 102.0 %all-gather.3.cloned.1.call-done = bf16[768,3584]{1,0:T(8,128)(2,1)} async-done(((bf16[768,896]{1,0:T(8,128)(2,1)}), bf16[768,3584]{1,0:T(8,128)(2,1)}) %all-gather.3.cloned.1.call-update) | async-done | bytes 5505040 | tf_op jit(solution)/shard_map/all_gather | solution.py:59
  156.6 0.0 copy-start
  156.6 0.0 copy-start.3
  156.6 6.1 %fusion.2 = f32[640,512]{1,0:T(8,128)S(1)} fusion(bf16[768,3584]{1,0:T(8,128)(2,1)} %all-gather.3.cloned.1.call-done, bf16[1,3584,512]{2,1,0:T(8,128)(2,1)} %param.12), kind=kOutput, calls=%fused_computation.4 | convolution fusion | flops 2348810240 | bytes 9568256 | tf_op jit(solution)/shard_map/dot_general | solution.py:10
  162.7 0.0 copy-done
  162.7 0.0 copy-done.3
  162.7 0.0 copy-start.6
  162.7 0.6 fusion.34
  163.3 1.4 copy-done.6
  164.7 0.0 copy-start.7
  164.7 2.6 fusion.24
  167.4 0.0 copy-done.7
  167.4 0.6 fusion.31
  168.0 0.9 pad_maximum_fusion.1
  169.0 0.0 all-gather.5.cloned.1.call-update
  169.0 61.9 %all-gather.5.cloned.1.call-done = bf16[768,2048]{1,0:T(8,128)(2,1)} async-done(((bf16[768,512]{1,0:T(8,128)(2,1)}), bf16[768,2048]{1,0:T(8,128)(2,1)}) %all-gather.5.cloned.1.call-update) | async-done | bytes 3145744 | tf_op jit(solution)/shard_map/all_gather | solution.py:69
  230.9 5.7 %fusion.11 = bf16[640,896]{1,0:T(8,128)(2,1)S(1)} fusion(bf16[1,2048,896]{2,1,0:T(8,128)(2,1)} %param.14, bf16[768,2048]{1,0:T(8,128)(2,1)} %all-gather.5.cloned.1.call-done), kind=kOutput, calls=%fused_computation.14 | convolution fusion | flops 2349383680 | bytes 7438336 | tf_op jit(solution)/shard_map/dot_general | solution.py:10
  236.6 0.4 reshape.113
  237.0 18.0 %all_to_all.22 = bf16[4,2,71680]{2,1,0:T(2,128)(2,1)S(1)} all-to-all(bf16[4,2,71680]{2,1,0:T(2,128)(2,1)S(1)} %reshape.113), channel_id=1, replica_groups=mesh['ctx'=4,'node'=4,'local'=2] {'node'}, dimensions={0} | all-to-all | bytes 2293760 | tf_op jit(solution)/shard_map/all_to_all | solution.py:75
  255.0 0.0 copy-start.4
  255.0 0.0 copy-start.5
  255.0 1.6 copy.49
  256.6 3.8 %all-to-all-start.3 = ((bf16[4,2,71680]{2,0,1:T(4,128)(2,1)}), bf16[4,2,71680]{2,0,1:T(4,128)(2,1)S(1)}, u32[]{:S(2)}, u32[]{:S(2)}) async-start(bf16[4,2,71680]{2,0,1:T(4,128)(2,1)} %copy.49), calls=%async_computation.3 | async-start | bytes 2293760 | tf_op jit(solution)/shard_map/all_to_all | solution.py:74
  260.4 0.0 copy-done.4
  260.4 0.1 copy.51
  260.5 0.1 mul.67
  260.6 0.1 copy.47
  260.7 0.0 copy-done.5
  260.8 0.1 copy.48
  260.9 13.9 %all-to-all-done.3 = bf16[4,2,71680]{2,0,1:T(4,128)(2,1)S(1)} async-done(((bf16[4,2,71680]{2,0,1:T(4,128)(2,1)}), bf16[4,2,71680]{2,0,1:T(4,128)(2,1)S(1)}, u32[]{:S(2)}, u32[]{:S(2)}) %all-to-all-start.3) | async-done | bytes 1146912 | tf_op jit(solution)/shard_map/all_to_all | solution.py:74
  274.9 1.2 copy.50
  276.0 0.8 reshape.114
  276.9 2.1 gather_fusion.1
  278.9 0.5 reshape.115
  279.4 0.0 copy-start.1
  279.4 2.3 fusion.16
  281.7 1.3 convert_reduce_fusion
  283.0 0.0 copy-done.1
  283.0 2.5 fusion.30
  (12 shorter events, 0.1 us)
Async XLA Ops:
  6.5 150.0 %all-gather.3.cloned.1.call-start = ((), (), s32[]{:S(2)}) async-start(), calls=%async_computation.4 | async-start | bytes 6881280 | tf_op jit(solution)/shard_map/all_gather | solution.py:59
  51.3 2.0 copy-start.2
  54.5 176.4 %all-gather.5.cloned.1.call-start = ((), (), s32[]{:S(2)}) async-start(), calls=%async_computation.5 | async-start | bytes 3932160 | tf_op jit(solution)/shard_map/all_gather | solution.py:69
  156.6 6.1 %copy-start = (bf16[3584,512]{1,0:T(8,128)(2,1)S(1)}, bf16[3584,512]{1,0:T(8,128)(2,1)}, u32[]{:S(2)}) copy-start(bf16[3584,512]{1,0:T(8,128)(2,1)} %param.15) | copy-start | bytes 11010052
  156.6 6.1 %copy-start.3 = (bf16[768,3584]{1,0:T(8,128)(2,1)S(1)}, bf16[768,3584]{1,0:T(8,128)(2,1)}, u32[]{:S(2)}) copy-start(bf16[768,3584]{1,0:T(8,128)(2,1)} %all-gather.3.cloned.1.call-done) | copy-start | bytes 16515076
  162.7 2.0 copy-start.6
  164.7 2.7 copy-start.7
  255.0 5.4 %copy-start.4 = (s32[128,4]{0,1:T(4,128)S(1)}, s32[128,4]{0,1:T(4,128)}, u32[]{:S(2)}) copy-start(s32[128,4]{0,1:T(4,128)} %param.10) | copy-start | bytes 6148
  255.0 5.7 %copy-start.5 = (f32[128,4]{0,1:T(4,128)S(1)}, f32[128,4]{0,1:T(4,128)}, u32[]{:S(2)}) copy-start(f32[128,4]{0,1:T(4,128)} %param.11) | copy-start | bytes 6148
  256.6 18.3 %all-to-all-start.3 = ((bf16[4,2,71680]{2,0,1:T(4,128)(2,1)}), bf16[4,2,71680]{2,0,1:T(4,128)(2,1)S(1)}, u32[]{:S(2)}, u32[]{:S(2)}) async-start(bf16[4,2,71680]{2,0,1:T(4,128)(2,1)} %copy.49), calls=%async_computation.3 | async-start | bytes 2293760 | tf_op jit(solution)/shard_map/all_to_all | solution.py:74
  279.4 3.6 %copy-start.1 = (bf16[2048,896]{1,0:T(8,128)(2,1)S(1)}, bf16[2048,896]{1,0:T(8,128)(2,1)}, u32[]{:S(2)}) copy-start(bf16[2048,896]{1,0:T(8,128)(2,1)} %param.17) | copy-start | bytes 11010052
Sparse Core Ops, SparseCore 0:
  54.6 101.8 all-gather.2
  169.1 61.7 all-gather.4
where the time goes:
time: 293 us; the launch traced here: 292 us
  waiting for transfers between devices  178 us (61%)
  blocking collectives  54.7 us (19%)
  matrix products  20.5 us (7%)
  local copies, waits for them, and re-layouts  16.5 us (6%)
  between operations  13.7 us (5%)
  other arithmetic  5.24 us (2%)
  starting transfers between devices  3.82 us (1%)
    all_gather x1, waiting for transfers between devices, local(): segment = lax.all_gather(stacked, 'ctx', axis=1, tiled=True)  102 us
    all_gather x1, waiting for transfers between devices, local(): segment = lax.all_gather(hidden_stack, 'ctx', axis=1, tiled=True)  61.9 us
    all_to_all x1, blocking collectives, local(): lax.all_to_all(send_rows, 'node', split_axis=0, concat_axis=0, tiled=True)  19.6 us
    dot_general x6, matrix products, matmul(): return jnp.dot(left_side, right_side, preferred_element_type=jnp.float32)  18.2 us
    all_to_all x1, blocking collectives, local(): lax.all_to_all(sendback, 'node', split_axis=0, concat_axis=0, tiled=True)  18 us
    all_to_all x1, blocking collectives, local(): lax.all_to_all(lax.all_to_all(send_rows, 'node', split_axis=0, concat_axi...  17.1 us
    all_to_all x1, waiting for transfers between devices, local(): lax.all_to_all(lax.all_to_all(sendback, 'node', split_axis=0, concat_axis...  13.9 us
  transfers between devices with their start and end apart: 3, of which 3 were waited for; matrix products, arithmetic and copies ran while one was open for 0% of the time, Pallas kernels for 0%

commit v1 on v0

--- a/solution.py
+++ b/solution.py
@@ -1,16 +1,20 @@
 import jax
 import jax.numpy as jnp
 from jax import lax
+from jax.experimental import pallas as pl
+from jax.experimental.pallas import tpu as pltpu
 from jax.sharding import PartitionSpec as P
 
 route_scale = 2.5
+MESH = pl.DeviceIdType.MESH
+VMEM_BYTES = 64000 * 1024
 
 
 def matmul(left_side, right_side):
     return jnp.dot(left_side, right_side, preferred_element_type=jnp.float32)
 
 
-def local(
+def exchange(
     tokens, expert_ids, route_scores, w_gate, w_up, w_down, shared_gate, shared_up, shared_down
 ):
     tok_count = tokens.shape[0]
@@ -90,6 +94,459 @@
     return mixed.astype(jnp.bfloat16)
 
 
+def column_tiles(width, tile, visit):
+    whole = width // tile
+    if whole == 1:
+        visit(0, tile)
+    elif whole > 1:
+
+        def step(index, carry):
+            visit(pl.multiple_of(index * tile, tile), tile)
+            return carry
+
+        lax.fori_loop(0, whole, step, 0)
+    if width % tile:
+        visit(whole * tile, width % tile)
+
+
+def cube_kernel(
+    sizes,
+    tok_in,
+    meta_in,
+    wg_in,
+    wu_in,
+    wd_in,
+    sg_in,
+    su_in,
+    sd_in,
+    out_ref,
+    tok,
+    meta,
+    wg,
+    wu,
+    wd,
+    sg,
+    su,
+    sd,
+    rows_in,
+    hid_s,
+    hid,
+    part,
+    got,
+    total,
+    loc_sem,
+    z_send,
+    z_recv,
+    b_send,
+    b_recv,
+    m_send,
+    m_recv,
+    p_send,
+    p_recv,
+):
+    ctx_count, group_count, member_count, cap = sizes
+    c = lax.axis_index("ctx")
+    n = lax.axis_index("node")
+    l = lax.axis_index("local")
+    last = ctx_count - 1
+    tok_count = tok.shape[2]
+    feat = tok.shape[3]
+    width = wg.shape[1]
+    out_width = wd.shape[1]
+    slots = range(1, tok.shape[0])
+
+    def peer(slot):
+        node = n
+        if slot & 1:
+            node = node + 1 - 2 * lax.rem(node, 2)
+        if slot & 4:
+            node = lax.rem(node + group_count // 2, group_count)
+        member = lax.rem(l + 1, member_count) if slot & 2 else l
+        return {"node": node, "local": member}
+
+    first = pltpu.make_async_copy(tok_in, tok.at[0, c], loc_sem.at[0])
+    first.start()
+    first_meta = pltpu.make_async_copy(meta_in, meta.at[0], loc_sem.at[1])
+    first_meta.start()
+
+    barrier = pltpu.get_barrier_semaphore()
+    for slot in slots:
+        pl.semaphore_signal(barrier, inc=1, device_id=peer(slot), device_id_type=MESH)
+
+    @pl.when(c > 0)
+    def _():
+        pl.semaphore_signal(barrier, inc=1, device_id={"ctx": c - 1}, device_id_type=MESH)
+
+    @pl.when(c < last)
+    def _():
+        pl.semaphore_signal(barrier, inc=1, device_id={"ctx": c + 1}, device_id_type=MESH)
+
+    loads = []
+    for index, (src, dst) in enumerate(
+        ((sg_in, sg), (su_in, su), (wg_in, wg), (wu_in, wu), (sd_in, sd), (wd_in, wd))
+    ):
+        loads.append(pltpu.make_async_copy(src, dst, loc_sem.at[2 + index]))
+
+    inner = (c > 0) & (c < last)
+
+    @pl.when(inner)
+    def _():
+        pl.semaphore_wait(barrier, len(slots) + 2)
+
+    @pl.when(jnp.logical_not(inner))
+    def _():
+        pl.semaphore_wait(barrier, len(slots) + 1)
+
+    first.wait()
+    first_meta.wait()
+
+    def piece(chunk, shard):
+        if chunk == 0:
+            return tok.at[0, shard]
+        if chunk == 1:
+            return hid_s.at[shard]
+        return hid.at[chunk - 2, shard]
+
+    def line(chunk, depth, way, shard, target):
+        return pltpu.make_async_remote_copy(
+            src_ref=piece(chunk, shard),
+            dst_ref=piece(chunk, shard),
+            send_sem=z_send.at[way, depth, chunk],
+            recv_sem=z_recv.at[way, depth, chunk],
+            device_id={"ctx": target},
+            device_id_type=MESH,
+        )
+
+    def line_send(chunk, depth, finish=False):
+        for way in (0, 1):
+            shard, target = (c - depth, c + 1) if way == 0 else (c + depth, c - 1)
+            ready = (c >= depth) & (c < last) if way == 0 else (c + depth <= last) & (c > 0)
+
+            @pl.when(ready)
+            def _():
+                copy = line(chunk, depth, way, shard, target)
+                if finish:
+                    copy.wait_send()
+                else:
+                    copy.start()
+
+    def line_take(chunk, depth, then=None):
+        for way in (0, 1):
+            shard = c - 1 - depth if way == 0 else c + 1 + depth
+            ready = shard >= 0 if way == 0 else shard <= last
+
+            @pl.when(ready)
+            def _():
+                source = c - 1 if way == 0 else c + 1
+                line(chunk, depth, way, shard, source).wait_recv()
+                target = c + 1 if way == 0 else c - 1
+                if depth < last - 1:
+
+                    @pl.when(target < ctx_count if way == 0 else target >= 0)
+                    def _():
+                        line(chunk, depth + 1, way, shard, target).start()
+
+                if then is not None:
+                    then(shard)
+
+    def hand(src_slot, dst_slot, shard, over):
+        return pltpu.make_async_remote_copy(
+            src_ref=tok.at[src_slot, shard],
+            dst_ref=tok.at[dst_slot, shard],
+            send_sem=b_send.at[dst_slot, shard],
+            recv_sem=b_recv.at[dst_slot, shard],
+            device_id=peer(over),
+            device_id_type=MESH,
+        )
+
+    def spread(shard):
+        hand(0, 2, shard, 2).start()
+        hand(0, 4, shard, 4).start()
+        hand(0, 1, shard, 1).start()
+
+    line_send(0, 0)
+    spread(c)
+    greet = []
+    for slot in slots:
+        greet.append(
+            pltpu.make_async_remote_copy(
+                src_ref=meta.at[0],
+                dst_ref=meta.at[slot],
+                send_sem=m_send.at[slot],
+                recv_sem=m_recv.at[slot],
+                device_id=peer(slot),
+                device_id_type=MESH,
+            )
+        )
+        greet[-1].start()
+    for load in loads:
+        load.start()
+    for depth in range(last):
+        line_take(0, depth, spread)
+
+    rank_of = lambda slot: meta[slot, pl.ds(n, 1), :]
+    weight_of = lambda slot: meta[slot, pl.ds(group_count + n * member_count + l, 1), :]
+
+    def pick(row, slot):
+        spots = lax.broadcasted_iota(jnp.int32, (cap, tok_count), 0).astype(jnp.float32)
+        mask = jnp.where(spots == rank_of(slot), 1.0, 0.0).astype(jnp.bfloat16)
+
+        def step(shard, carry):
+            chosen = matmul(mask, tok[slot, shard]).astype(jnp.bfloat16)
+            rows_in[row : row + cap, pl.ds(pl.multiple_of(shard * feat, 128), feat)] = chosen
+            return carry
+
+        lax.fori_loop(0, ctx_count, step, 0)
+
+    def hidden(count, gate, up, target):
+        def visit(start, size):
+            cols = pl.ds(start, size)
+            g = matmul(rows_in[0:count, :], gate[:, cols])
+            u = matmul(rows_in[0:count, :], up[:, cols])
+            target[:, cols] = (g / (1.0 + jnp.exp(-g)) * u).astype(jnp.bfloat16)
+
+        column_tiles(width, 256, visit)
+
+    pairs = ((2, 3), (4, 5), (6, 7), (0, 1))
+
+    def compute(index):
+        for place, slot in enumerate(pairs[index]):
+            pick(place * cap, slot)
+        hidden(2 * cap, wg, wu, hid.at[index, c])
+
+    half = ctx_count // 2
+
+    def take(slot, shard):
+        hand(0, slot, shard, 1).wait_recv()
+
+    for shard in range(ctx_count):
+        rows_in[0:tok_count, shard * feat : (shard + 1) * feat] = tok[0, shard]
+    loads[0].wait()
+    loads[1].wait()
+    hidden(tok_count, sg, su, hid_s.at[c])
+    line_send(1, 0)
+
+    for shard in range(ctx_count):
+        take(2, shard)
+        hand(2, 3, shard, 1).start()
+        if shard < half:
+            hand(2, 6, shard, 4).start()
+        take(4, shard)
+        hand(4, 5, shard, 1).start()
+        if shard >= half:
+            hand(4, 6, shard, 2).start()
+    for copy in greet:
+        copy.wait_recv()
+    loads[2].wait()
+    loads[3].wait()
+    for shard in range(ctx_count):
+        take(1, shard)
+    compute(3)
+    for shard in range(ctx_count):
+        take(3, shard)
+    compute(0)
+    line_send(2, 0)
+    line_take(1, 0)
+    for shard in range(ctx_count):
+        take(5, shard)
+    compute(1)
+    line_send(3, 0)
+    line_take(2, 0)
+    line_take(1, 1)
+    for shard in range(ctx_count):
+        take(6, shard)
+        hand(6, 7, shard, 1).start()
+    for shard in range(ctx_count):
+        take(7, shard)
+    compute(2)
+    line_send(4, 0)
+    line_send(5, 0)
+    line_take(3, 0)
+    line_take(2, 1)
+    line_take(1, 2)
+
+    loads[4].wait()
+    loads[5].wait()
+
+    def product(chunk, down, cols):
+        value = matmul(piece(chunk, 0)[...], down[0:width, cols])
+        for shard in range(1, ctx_count):
+            value = value + matmul(
+                piece(chunk, shard)[...], down[shard * width : (shard + 1) * width, cols]
+            )
+        return value
+
+    def shared_down(start, size):
+        cols = pl.ds(start, size)
+        total[:, cols] = product(1, sd, cols)
+
+    column_tiles(out_width, 256, shared_down)
+
+    sends = []
+
+    def finish(index):
+        weights = []
+        for slot in pairs[index]:
+            spots = lax.broadcasted_iota(jnp.int32, (tok_count, tok_count), 0).astype(jnp.float32)
+            mask = jnp.where(spots == rank_of(slot), weight_of(slot), 0.0)
+            weights.append(jnp.transpose(mask)[:, 0:cap].astype(jnp.bfloat16))
+
+        def visit(start, size):
+            cols = pl.ds(start, size)
+            rows = product(index + 2, wd, cols).astype(jnp.bfloat16)
+            for place, slot in enumerate(pairs[index]):
+                value = matmul(weights[place], rows[place * cap : (place + 1) * cap])
+                if slot == 0:
+                    total[:, cols] += value
+                else:
+                    part[slot - 1, :, cols] = value.astype(jnp.bfloat16)
+
+        column_tiles(out_width, 256, visit)
+        for slot in pairs[index]:
+            if slot:
+                sends.append(
+                    pltpu.make_async_remote_copy(
+                        src_ref=part.at[slot - 1],
+                        dst_ref=got.at[slot - 1],
+                        send_sem=p_send.at[slot],
+                        recv_sem=p_recv.at[slot],
+                        device_id=peer(slot),
+                        device_id_type=MESH,
+                    )
+                )
+                sends[-1].start()
+
+    line_take(4, 0)
+    line_take(5, 0)
+    line_take(3, 1)
+    line_take(2, 2)
+    finish(0)
+    line_take(4, 1)
+    line_take(5, 1)
+    line_take(3, 2)
+    finish(1)
+    line_take(4, 2)
+    finish(2)
+    for copy in sends[:4]:
+        copy.wait_recv()
+
+    def gather_some(start, size):
+        cols = pl.ds(start, size)
+        value = total[:, cols]
+        for slot in (2, 3, 4, 5):
+            value = value + got[slot - 1, :, cols].astype(jnp.float32)
+        total[:, cols] = value
+
+    column_tiles(out_width, 256, gather_some)
+    line_take(5, 2)
+    finish(3)
+    for copy in sends[4:]:
+        copy.wait_recv()
+
+    def gather_rest(start, size):
+        cols = pl.ds(start, size)
+        value = total[:, cols]
+        for slot in (6, 7, 1):
+            value = value + got[slot - 1, :, cols].astype(jnp.float32)
+        out_ref[:, cols] = value.astype(jnp.bfloat16)
+
+    column_tiles(out_width, 256, gather_rest)
+
+    for copy in sends + greet:
+        copy.wait_send()
+    for chunk in range(6):
+        for depth in range(last):
+            line_send(chunk, depth, finish=True)
+    for shard in range(ctx_count):
+        for slot in (1, 2, 3, 4, 5, 6, 7):
+            hand(0, slot, shard, 1).wait_send()
+
+
+def cube(
+    tokens, expert_ids, route_scores, w_gate, w_up, w_down, shared_gate, shared_up, shared_down
+):
+    ctx_count = lax.axis_size("ctx")
+    group_count = lax.axis_size("node")
+    member_count = lax.axis_size("local")
+    expert_count = group_count * member_count
+    tok_count, feat = tokens.shape
+    cap = (10 * tok_count + 4 * group_count - 1) // (4 * group_count)
+    hidden_units, out_width = w_down.shape[1:]
+    width = w_gate.shape[2]
+    scaled = route_scale * route_scores / jnp.sum(route_scores, axis=1, keepdims=True)
+    gate_weights = lax.optimization_barrier(scaled.astype(jnp.bfloat16)).astype(jnp.float32)
+    ids = expert_ids.T
+    gates = gate_weights.T
+    experts = jnp.arange(expert_count, dtype=jnp.int32)
+    weights = jnp.sum(
+        jnp.where(ids[:, None, :] == experts[None, :, None], gates[:, None, :], 0.0), axis=0
+    )
+    groups = jnp.arange(group_count, dtype=jnp.int32)
+    member = jnp.any((ids // member_count)[:, None, :] == groups[None, :, None], axis=0)
+    span = jnp.arange(tok_count, dtype=jnp.int32)
+    earlier = (span[:, None] < span[None, :]).astype(jnp.bfloat16)
+    rank = jnp.where(member, matmul(member.astype(jnp.bfloat16), earlier), -1.0)
+    meta_rows = group_count + expert_count
+    pad = -meta_rows % 8
+    meta = jnp.concatenate([rank, weights, jnp.zeros((pad, tok_count), jnp.float32)], axis=0)
+    slots = 2 * group_count
+    bf16 = jnp.bfloat16
+    rows = max(2 * cap, tok_count)
+    anywhere = pl.BlockSpec(memory_space=pl.ANY)
+    dma = pltpu.SemaphoreType.DMA
+    kernel = lambda *refs: cube_kernel((ctx_count, group_count, member_count, cap), *refs)
+    return pl.pallas_call(
+        kernel,
+        out_shape=jax.ShapeDtypeStruct((tok_count, out_width), bf16),
+        in_specs=[anywhere] * 8,
+        out_specs=pl.BlockSpec(memory_space=pltpu.VMEM),
+        scratch_shapes=[
+            pltpu.VMEM((slots, ctx_count, tok_count, feat), bf16),
+            pltpu.VMEM((slots,) + meta.shape, jnp.float32),
+            pltpu.VMEM(w_gate.shape[1:], bf16),
+            pltpu.VMEM(w_up.shape[1:], bf16),
+            pltpu.VMEM(w_down.shape[1:], bf16),
+            pltpu.VMEM(shared_gate.shape, bf16),
+            pltpu.VMEM(shared_up.shape, bf16),
+            pltpu.VMEM(shared_down.shape, bf16),
+            pltpu.VMEM((rows, ctx_count * feat), bf16),
+            pltpu.VMEM((ctx_count, tok_count, width), bf16),
+            pltpu.VMEM((4, ctx_count, 2 * cap, width), bf16),
+            pltpu.VMEM((slots - 1, tok_count, out_width), bf16),
+            pltpu.VMEM((slots - 1, tok_count, out_width), bf16),
+            pltpu.VMEM((tok_count, out_width), jnp.float32),
+            dma((8,)),
+            dma((2, ctx_count - 1, 6)),
+            dma((2, ctx_count - 1, 6)),
+            dma((slots, ctx_count)),
+            dma((slots, ctx_count)),
+            dma((slots,)),
+            dma((slots,)),
+            dma((slots,)),
+            dma((slots,)),
+        ],
+        compiler_params=pltpu.CompilerParams(
+            collective_id=0, has_side_effects=True, vmem_limit_bytes=VMEM_BYTES
+        ),
+    )(
+        tokens,
+        meta,
+        w_gate[0],
+        w_up[0],
+        w_down[0],
+        shared_gate,
+        shared_up,
+        shared_down,
+    )
+
+
+def local(tokens, expert_ids, *rest):
+    whole_groups = expert_ids.shape[1] == 2 * lax.axis_size("local")
+    if whole_groups and lax.axis_size("local") == 2 and lax.axis_size("node") == 4:
+        return cube(tokens, expert_ids, *rest)
+    return exchange(tokens, expert_ids, *rest)
+
+
 def solution(mesh):
     return jax.shard_map(
         local,

time: 293 us -> 109 us (0.37)
  waiting for transfers between devices: 178 us -> 0 us
  Pallas kernels: 0 us -> 104 us
  blocking collectives: 54.7 us -> 0 us
  matrix products: 20.5 us -> 0.13 us
  local copies, waits for them, and re-layouts: 16.5 us -> 1.72 us
  between operations: 13.7 us -> 0.01 us
  starting transfers between devices: 3.82 us -> 0 us
    all_gather x2 -> x0, waiting for transfers between devices: 164 us -> none  [the longest x1 102 us: local(): segment = lax.all_gather(stacked, 'ctx', axis=1, tiled=True)]
    pallas_call x0 -> x1, Pallas kernels: none -> 104 us  [cube(): pl.pallas_call(kernel, out_shape=jax.ShapeDtypeStruct((tok_count, out_wid...]
    all_to_all x3 -> x0, blocking collectives: 54.7 us -> none  [the longest x1 19.6 us: local(): lax.all_to_all(send_rows, 'node', split_axis=0, concat_axis=0, tiled=True)]
    dot_general x6 -> x1, matrix products: 18.2 us -> 0.13 us  [matmul(): return jnp.dot(left_side, right_side, preferred_element_type=jnp.float32)]
    all_to_all x1 -> x0, waiting for transfers between devices: 13.9 us -> none  [local(): lax.all_to_all(lax.all_to_all(sendback, 'node', split_axis=0, concat_axis...]
    gather x2 -> x0, local copies, waits for them, and re-layouts: 5.16 us -> none  [the longest x1 3.1 us: local(): padded_tokens[slot_token]]
    all_to_all x4 -> x0, local copies, waits for them, and re-layouts: 4.55 us -> none  [the longest x1 1.6 us: local(): lax.all_to_all(sendback, 'node', split_axis=0, concat_axis=0, tiled=True)]
    all_to_all x1 -> x0, starting transfers between devices: 3.78 us -> none  [local(): lax.all_to_all(lax.all_to_all(sendback, 'node', split_axis=0, concat_axis...]
  transfers between devices with their start and end apart: 3 -> 0, of which waited for: 3 -> 0; matrix products, arithmetic and copies ran while one was open for 0% -> 0% of each run, Pallas kernels for 0% -> 0%
where the time goes in v1:
time: 109 us
  Pallas kernels  104 us (95%)
  other arithmetic  3.46 us (3%)
  local copies, waits for them, and re-layouts  1.72 us (2%)
    pallas_call x1, Pallas kernels, cube(): pl.pallas_call(kernel, out_shape=jax.ShapeDtypeStruct((tok_count, out_wid...  104 us

profile of v1, /device:TPU:0, one launch (start us, length us, event | category | flops | bytes accessed | tf_op | source)
XLA Modules:
  0.0 109.2 jit_solution(16774355127901201438)
XLA Ops:
  0.0 0.7 reduce_sum.18
  0.7 0.7 fusion.2
  1.4 0.1 pad.2.clone
  1.5 0.7 select_reduce_fusion
  2.2 0.7 add_select_fusion
  2.9 0.1 convolution_select_fusion
  3.0 0.7 maximum_maximum_fusion.refs_1_
  3.7 103.9 %shard_map.91 = bf16[128,896]{1,0:T(8,128)(2,1)} custom-call(bf16[128,896]{1,0:T(8,128)(2,1)} %refs_0_.1, f32[16,128]{1,0:T(8,128)} %maximum_maximum_fusion.refs_1_, bf16[3584,512]{1,0:T(8,128)(2,1)} %bitcast.8, bf16[3584,512]{1,0:T(8,128)(2,1)} %bitcast.9, bf16[2048,896]{1,0:T(8,128)(2,1)} %bitcast.10, bf16[3584,512]{1,0:T(8,128)(2,1)} %refs_5_.1, ...), custom_call_target="tpu_custom_call" | custom-call | tf_op jit(solution)/shard_map/pallas_call | solution.py:498
  107.6 1.6 %copy.11 = bf16[128,896]{1,0:T(8,128)(2,1)} copy(bf16[128,896]{1,0:T(8,128)(2,1)} %shard_map.91) | data formatting | bytes 458752
  (3 shorter events, 0.0 us)

commit v2 on v1

--- a/solution.py
+++ b/solution.py
@@ -112,7 +112,8 @@
 def cube_kernel(
     sizes,
     tok_in,
-    meta_in,
+    ids_in,
+    scores_in,
     wg_in,
     wu_in,
     wd_in,
@@ -134,6 +135,8 @@
     part,
     got,
     total,
+    sum_g,
+    sum_u,
     loc_sem,
     z_send,
     z_recv,
@@ -166,8 +169,6 @@
 
     first = pltpu.make_async_copy(tok_in, tok.at[0, c], loc_sem.at[0])
     first.start()
-    first_meta = pltpu.make_async_copy(meta_in, meta.at[0], loc_sem.at[1])
-    first_meta.start()
 
     barrier = pltpu.get_barrier_semaphore()
     for slot in slots:
@@ -198,7 +199,6 @@
         pl.semaphore_wait(barrier, len(slots) + 1)
 
     first.wait()
-    first_meta.wait()
 
     def piece(chunk, shard):
         if chunk == 0:
@@ -266,6 +266,27 @@
 
     line_send(0, 0)
     spread(c)
+    for load in loads:
+        load.start()
+
+    scores = scores_in[...]
+    scaled = route_scale * scores / jnp.sum(scores, axis=1, keepdims=True)
+    gates = scaled.astype(jnp.bfloat16).astype(jnp.float32)
+    lane = lax.broadcasted_iota(jnp.int32, (tok_count, tok_count), 1)
+    named = jnp.zeros((tok_count, tok_count), jnp.float32)
+    for k in range(ids_in.shape[1]):
+        expert = ids_in[:, k : k + 1]
+        named = jnp.maximum(named, jnp.where(lane == expert // member_count, 1.0, 0.0))
+    table = jnp.where(lane < group_count, named, 0.0)
+    for k in range(ids_in.shape[1]):
+        expert = ids_in[:, k : k + 1]
+        table = table + jnp.where(lane == expert + group_count, gates[:, k : k + 1], 0.0)
+    table = jnp.transpose(table)[0 : meta.shape[1]]
+    before = lax.broadcasted_iota(jnp.int32, (tok_count, tok_count), 0) < lane
+    counts = matmul(table.astype(jnp.bfloat16), jnp.where(before, 1.0, 0.0).astype(jnp.bfloat16))
+    row = lax.broadcasted_iota(jnp.int32, table.shape, 0)
+    meta[0] = jnp.where(row < group_count, jnp.where(table > 0.5, counts, -1.0), table)
+
     greet = []
     for slot in slots:
         greet.append(
@@ -279,10 +300,30 @@
             )
         )
         greet[-1].start()
-    for load in loads:
-        load.start()
+
+    def shared_add(shard, fresh=False):
+        ins = pl.ds(pl.multiple_of(shard * feat, 128), feat)
+
+        def visit(start, size):
+            cols = pl.ds(start, size)
+            g = matmul(tok[0, shard], sg[ins, cols])
+            u = matmul(tok[0, shard], su[ins, cols])
+            sum_g[:, cols] = g if fresh else sum_g[:, cols] + g
+            sum_u[:, cols] = u if fresh else sum_u[:, cols] + u
+
+        column_tiles(width, 256, visit)
+
+    loads[0].wait()
+    loads[1].wait()
+    shared_add(c, True)
     for depth in range(last):
         line_take(0, depth, spread)
+        for shard in (c - 1 - depth, c + 1 + depth):
+
+            @pl.when((shard >= 0) & (shard <= last))
+            def _():
+                shared_add(shard)
+
 
     rank_of = lambda slot: meta[slot, pl.ds(n, 1), :]
     weight_of = lambda slot: meta[slot, pl.ds(group_count + n * member_count + l, 1), :]
@@ -319,13 +360,18 @@
     def take(slot, shard):
         hand(0, slot, shard, 1).wait_recv()
 
-    for shard in range(ctx_count):
-        rows_in[0:tok_count, shard * feat : (shard + 1) * feat] = tok[0, shard]
-    loads[0].wait()
-    loads[1].wait()
-    hidden(tok_count, sg, su, hid_s.at[c])
+    g = sum_g[...]
+    hid_s[c] = (g / (1.0 + jnp.exp(-g)) * sum_u[...]).astype(jnp.bfloat16)
     line_send(1, 0)
 
+    for copy in greet:
+        copy.wait_recv()
+    loads[2].wait()
+    loads[3].wait()
+    for shard in range(ctx_count):
+        take(1, shard)
+    compute(3)
+    line_take(1, 0)
     for shard in range(ctx_count):
         take(2, shard)
         hand(2, 3, shard, 1).start()
@@ -335,34 +381,16 @@
         hand(4, 5, shard, 1).start()
         if shard >= half:
             hand(4, 6, shard, 2).start()
-    for copy in greet:
-        copy.wait_recv()
-    loads[2].wait()
-    loads[3].wait()
-    for shard in range(ctx_count):
-        take(1, shard)
-    compute(3)
     for shard in range(ctx_count):
         take(3, shard)
     compute(0)
     line_send(2, 0)
-    line_take(1, 0)
+    line_take(1, 1)
     for shard in range(ctx_count):
         take(5, shard)
     compute(1)
     line_send(3, 0)
     line_take(2, 0)
-    line_take(1, 1)
-    for shard in range(ctx_count):
-        take(6, shard)
-        hand(6, 7, shard, 1).start()
-    for shard in range(ctx_count):
-        take(7, shard)
-    compute(2)
-    line_send(4, 0)
-    line_send(5, 0)
-    line_take(3, 0)
-    line_take(2, 1)
     line_take(1, 2)
 
     loads[4].wait()
@@ -416,15 +444,25 @@
                 )
                 sends[-1].start()
 
-    line_take(4, 0)
-    line_take(5, 0)
+    for shard in range(ctx_count):
+        take(6, shard)
+        hand(6, 7, shard, 1).start()
+    line_take(2, 1)
+    for shard in range(ctx_count):
+        take(7, shard)
+    compute(2)
+    line_send(4, 0)
+    line_take(3, 0)
     line_take(3, 1)
     line_take(2, 2)
     finish(0)
+    line_send(5, 0)
+    line_take(4, 0)
     line_take(4, 1)
-    line_take(5, 1)
     line_take(3, 2)
     finish(1)
+    line_take(5, 0)
+    line_take(5, 1)
     line_take(4, 2)
     finish(2)
     for copy in sends[:4]:
@@ -473,36 +511,22 @@
     cap = (10 * tok_count + 4 * group_count - 1) // (4 * group_count)
     hidden_units, out_width = w_down.shape[1:]
     width = w_gate.shape[2]
-    scaled = route_scale * route_scores / jnp.sum(route_scores, axis=1, keepdims=True)
-    gate_weights = lax.optimization_barrier(scaled.astype(jnp.bfloat16)).astype(jnp.float32)
-    ids = expert_ids.T
-    gates = gate_weights.T
-    experts = jnp.arange(expert_count, dtype=jnp.int32)
-    weights = jnp.sum(
-        jnp.where(ids[:, None, :] == experts[None, :, None], gates[:, None, :], 0.0), axis=0
-    )
-    groups = jnp.arange(group_count, dtype=jnp.int32)
-    member = jnp.any((ids // member_count)[:, None, :] == groups[None, :, None], axis=0)
-    span = jnp.arange(tok_count, dtype=jnp.int32)
-    earlier = (span[:, None] < span[None, :]).astype(jnp.bfloat16)
-    rank = jnp.where(member, matmul(member.astype(jnp.bfloat16), earlier), -1.0)
-    meta_rows = group_count + expert_count
-    pad = -meta_rows % 8
-    meta = jnp.concatenate([rank, weights, jnp.zeros((pad, tok_count), jnp.float32)], axis=0)
+    meta_rows = -(-(group_count + expert_count) // 16) * 16
     slots = 2 * group_count
     bf16 = jnp.bfloat16
     rows = max(2 * cap, tok_count)
     anywhere = pl.BlockSpec(memory_space=pl.ANY)
+    inside = pl.BlockSpec(memory_space=pltpu.VMEM)
     dma = pltpu.SemaphoreType.DMA
     kernel = lambda *refs: cube_kernel((ctx_count, group_count, member_count, cap), *refs)
     return pl.pallas_call(
         kernel,
         out_shape=jax.ShapeDtypeStruct((tok_count, out_width), bf16),
-        in_specs=[anywhere] * 8,
-        out_specs=pl.BlockSpec(memory_space=pltpu.VMEM),
+        in_specs=[anywhere, inside, inside] + [anywhere] * 6,
+        out_specs=inside,
         scratch_shapes=[
             pltpu.VMEM((slots, ctx_count, tok_count, feat), bf16),
-            pltpu.VMEM((slots,) + meta.shape, jnp.float32),
+            pltpu.VMEM((slots, meta_rows, tok_count), jnp.float32),
             pltpu.VMEM(w_gate.shape[1:], bf16),
             pltpu.VMEM(w_up.shape[1:], bf16),
             pltpu.VMEM(w_down.shape[1:], bf16),
@@ -515,6 +539,8 @@
             pltpu.VMEM((slots - 1, tok_count, out_width), bf16),
             pltpu.VMEM((slots - 1, tok_count, out_width), bf16),
             pltpu.VMEM((tok_count, out_width), jnp.float32),
+            pltpu.VMEM((tok_count, width), jnp.float32),
+            pltpu.VMEM((tok_count, width), jnp.float32),
             dma((8,)),
             dma((2, ctx_count - 1, 6)),
             dma((2, ctx_count - 1, 6)),
@@ -530,7 +556,8 @@
         ),
     )(
         tokens,
-        meta,
+        expert_ids,
+        route_scores,
         w_gate[0],
         w_up[0],
         w_down[0],

time: 109 us -> 104 us (0.954)
  Pallas kernels: 104 us -> 99.7 us
  other arithmetic: 3.46 us -> 0 us
  local copies, waits for them, and re-layouts: 1.72 us -> 4.47 us
    pallas_call x1, Pallas kernels: 104 us -> 99.7 us  [cube(): pl.pallas_call(kernel, out_shape=jax.ShapeDtypeStruct((tok_count, out_wid...]
    unnamed x1 -> x3, local copies, waits for them, and re-layouts: 1.65 us -> 4.47 us
    reduce_sum x2 -> x0, other arithmetic: 1.39 us -> none  [the longest x1 0.7 us: cube(): jnp.sum(route_scores, axis=1, keepdims=True)]
where the time goes in v2:
time: 104 us
  Pallas kernels  99.7 us (96%)
  local copies, waits for them, and re-layouts  4.47 us (4%)
    pallas_call x1, Pallas kernels, cube(): pl.pallas_call(kernel, out_shape=jax.ShapeDtypeStruct((tok_count, out_wid...  99.7 us
    unnamed x3, local copies, waits for them, and re-layouts  4.47 us

profile of v2, /device:TPU:0, one launch (start us, length us, event | category | flops | bytes accessed | tf_op | source)
XLA Modules:
  0.0 104.1 jit_solution(2796296952690755252)
XLA Ops:
  0.0 1.4 %copy.10.refs_1_ = s32[128,4]{1,0:T(8,128)} copy(s32[128,4]{0,1:T(4,128)} %param.10) | data formatting | bytes 4096 | tf_op args[1]
  1.4 1.4 %copy.11.refs_2_ = f32[128,4]{1,0:T(8,128)} copy(f32[128,4]{0,1:T(4,128)} %param.11) | data formatting | bytes 4096 | tf_op args[2]
  2.8 99.7 %shard_map.91 = bf16[128,896]{1,0:T(8,128)(2,1)} custom-call(bf16[128,896]{1,0:T(8,128)(2,1)} %refs_0_.1, s32[128,4]{1,0:T(8,128)} %copy.10.refs_1_, f32[128,4]{1,0:T(8,128)} %copy.11.refs_2_, bf16[3584,512]{1,0:T(8,128)(2,1)} %bitcast.3, bf16[3584,512]{1,0:T(8,128)(2,1)} %bitcast.4, bf16[2048,896]{1,0:T(8,128)(2,1)} %bitcast.5, bf16[3584,512]{1,0:T(8,128)(2,1)} %refs_6_.1, ...), custom_call_target="tpu_custom_call" | custom-call | tf_op jit(solution)/shard_map/pallas_call | solution.py:522
  102.5 1.6 %copy.13 = bf16[128,896]{1,0:T(8,128)(2,1)} copy(bf16[128,896]{1,0:T(8,128)(2,1)} %shard_map.91) | data formatting | bytes 458752

commit v3 on v2

--- a/solution.py
+++ b/solution.py
@@ -137,6 +137,7 @@
     total,
     sum_g,
     sum_u,
+    hold,
     loc_sem,
     z_send,
     z_recv,
@@ -270,22 +271,19 @@
         load.start()
 
     scores = scores_in[...]
-    scaled = route_scale * scores / jnp.sum(scores, axis=1, keepdims=True)
+    scaled = route_scale * scores / jnp.sum(scores, axis=0, keepdims=True)
     gates = scaled.astype(jnp.bfloat16).astype(jnp.float32)
-    lane = lax.broadcasted_iota(jnp.int32, (tok_count, tok_count), 1)
-    named = jnp.zeros((tok_count, tok_count), jnp.float32)
-    for k in range(ids_in.shape[1]):
-        expert = ids_in[:, k : k + 1]
-        named = jnp.maximum(named, jnp.where(lane == expert // member_count, 1.0, 0.0))
-    table = jnp.where(lane < group_count, named, 0.0)
-    for k in range(ids_in.shape[1]):
-        expert = ids_in[:, k : k + 1]
-        table = table + jnp.where(lane == expert + group_count, gates[:, k : k + 1], 0.0)
-    table = jnp.transpose(table)[0 : meta.shape[1]]
-    before = lax.broadcasted_iota(jnp.int32, (tok_count, tok_count), 0) < lane
-    counts = matmul(table.astype(jnp.bfloat16), jnp.where(before, 1.0, 0.0).astype(jnp.bfloat16))
-    row = lax.broadcasted_iota(jnp.int32, table.shape, 0)
-    meta[0] = jnp.where(row < group_count, jnp.where(table > 0.5, counts, -1.0), table)
+    row = lax.broadcasted_iota(jnp.int32, meta.shape[1:], 0)
+    named = jnp.zeros(row.shape, jnp.float32)
+    table = jnp.zeros(row.shape, jnp.float32)
+    for k in range(ids_in.shape[0]):
+        expert = ids_in[k : k + 1, :]
+        named = jnp.where(row == expert // member_count, 1.0, named)
+        table = table + jnp.where(row == expert + group_count, gates[k : k + 1, :], 0.0)
+    square = (tok_count, tok_count)
+    before = lax.broadcasted_iota(jnp.int32, square, 0) < lax.broadcasted_iota(jnp.int32, square, 1)
+    counts = matmul(named.astype(jnp.bfloat16), jnp.where(before, 1.0, 0.0).astype(jnp.bfloat16))
+    meta[0] = jnp.where(row < group_count, jnp.where(named > 0.5, counts, -1.0), table)
 
     greet = []
     for slot in slots:
@@ -410,7 +408,18 @@
 
     column_tiles(out_width, 256, shared_down)
 
-    sends = []
+    sends = {}
+
+    def ship(slot, over):
+        sends[slot] = pltpu.make_async_remote_copy(
+            src_ref=part.at[slot - 1],
+            dst_ref=got.at[slot - 1],
+            send_sem=p_send.at[slot],
+            recv_sem=p_recv.at[slot],
+            device_id=peer(over),
+            device_id_type=MESH,
+        )
+        sends[slot].start()
 
     def finish(index):
         weights = []
@@ -426,23 +435,25 @@
                 value = matmul(weights[place], rows[place * cap : (place + 1) * cap])
                 if slot == 0:
                     total[:, cols] += value
+                elif place == 0:
+                    hold[:, cols] = value
                 else:
                     part[slot - 1, :, cols] = value.astype(jnp.bfloat16)
 
         column_tiles(out_width, 256, visit)
-        for slot in pairs[index]:
-            if slot:
-                sends.append(
-                    pltpu.make_async_remote_copy(
-                        src_ref=part.at[slot - 1],
-                        dst_ref=got.at[slot - 1],
-                        send_sem=p_send.at[slot],
-                        recv_sem=p_recv.at[slot],
-                        device_id=peer(slot),
-                        device_id_type=MESH,
-                    )
-                )
-                sends[-1].start()
+        ship(pairs[index][1], 1)
+
+    def forward(index):
+        slot, other = pairs[index]
+        sends[other].wait_recv()
+
+        def visit(start, size):
+            cols = pl.ds(start, size)
+            value = hold[:, cols] + got[other - 1, :, cols].astype(jnp.float32)
+            part[slot - 1, :, cols] = value.astype(jnp.bfloat16)
+
+        column_tiles(out_width, 256, visit)
+        ship(slot, slot)
 
     for shard in range(ctx_count):
         take(6, shard)
@@ -458,39 +469,42 @@
     finish(0)
     line_send(5, 0)
     line_take(4, 0)
+    forward(0)
     line_take(4, 1)
     line_take(3, 2)
     finish(1)
     line_take(5, 0)
+    forward(1)
     line_take(5, 1)
     line_take(4, 2)
     finish(2)
-    for copy in sends[:4]:
-        copy.wait_recv()
+    forward(2)
+    for slot in (2, 4):
+        sends[slot].wait_recv()
 
     def gather_some(start, size):
         cols = pl.ds(start, size)
         value = total[:, cols]
-        for slot in (2, 3, 4, 5):
+        for slot in (2, 4):
             value = value + got[slot - 1, :, cols].astype(jnp.float32)
         total[:, cols] = value
 
     column_tiles(out_width, 256, gather_some)
     line_take(5, 2)
     finish(3)
-    for copy in sends[4:]:
-        copy.wait_recv()
+    for slot in (6, 1):
+        sends[slot].wait_recv()
 
     def gather_rest(start, size):
         cols = pl.ds(start, size)
         value = total[:, cols]
-        for slot in (6, 7, 1):
+        for slot in (6, 1):
             value = value + got[slot - 1, :, cols].astype(jnp.float32)
         out_ref[:, cols] = value.astype(jnp.bfloat16)
 
     column_tiles(out_width, 256, gather_rest)
 
-    for copy in sends + greet:
+    for copy in list(sends.values()) + greet:
         copy.wait_send()
     for chunk in range(6):
         for depth in range(last):
@@ -541,6 +555,7 @@
             pltpu.VMEM((tok_count, out_width), jnp.float32),
             pltpu.VMEM((tok_count, width), jnp.float32),
             pltpu.VMEM((tok_count, width), jnp.float32),
+            pltpu.VMEM((tok_count, out_width), jnp.float32),
             dma((8,)),
             dma((2, ctx_count - 1, 6)),
             dma((2, ctx_count - 1, 6)),
@@ -556,8 +571,8 @@
         ),
     )(
         tokens,
-        expert_ids,
-        route_scores,
+        expert_ids.T,
+        route_scores.T,
         w_gate[0],
         w_up[0],
         w_down[0],

time: 104 us -> 92.5 us (0.89)
  Pallas kernels: 99.7 us -> 90.5 us
  local copies, waits for them, and re-layouts: 4.47 us -> 1.65 us
    pallas_call x1, Pallas kernels: 99.7 us -> 90.5 us  [cube(): pl.pallas_call(kernel, out_shape=jax.ShapeDtypeStruct((tok_count, out_wid...]
    unnamed x3 -> x1, local copies, waits for them, and re-layouts: 4.47 us -> 1.65 us
where the time goes in v3:
time: 92.5 us; the launch traced here: 92.2 us
  Pallas kernels  90.5 us (98%)
  local copies, waits for them, and re-layouts  1.65 us (2%)
    pallas_call x1, Pallas kernels, cube(): pl.pallas_call(kernel, out_shape=jax.ShapeDtypeStruct((tok_count, out_wid...  90.5 us

profile of v3, /device:TPU:0, one launch (start us, length us, event | category | flops | bytes accessed | tf_op | source)
XLA Modules:
  0.0 92.2 jit_solution(16793175301058145847)
XLA Ops:
  0.0 90.5 %shard_map.91 = bf16[128,896]{1,0:T(8,128)(2,1)} custom-call(bf16[128,896]{1,0:T(8,128)(2,1)} %refs_0_.1, s32[4,128]{1,0:T(4,128)} %bitcast.8, f32[4,128]{1,0:T(4,128)} %bitcast.9, bf16[3584,512]{1,0:T(8,128)(2,1)} %bitcast.5, bf16[3584,512]{1,0:T(8,128)(2,1)} %bitcast.6, bf16[2048,896]{1,0:T(8,128)(2,1)} %bitcast.7, bf16[3584,512]{1,0:T(8,128)(2,1)} %refs_6_.1, ...), custom_call_target="tpu_custom_call" | custom-call | tf_op jit(solution)/shard_map/pallas_call | solution.py:536
  90.5 1.6 %copy.11 = bf16[128,896]{1,0:T(8,128)(2,1)} copy(bf16[128,896]{1,0:T(8,128)(2,1)} %shard_map.91) | data formatting | bytes 458752

commit v4 on v3

--- a/solution.py
+++ b/solution.py
@@ -369,6 +369,7 @@
     for shard in range(ctx_count):
         take(1, shard)
     compute(3)
+    line_send(5, 0)
     line_take(1, 0)
     for shard in range(ctx_count):
         take(2, shard)
@@ -467,7 +468,6 @@
     line_take(3, 1)
     line_take(2, 2)
     finish(0)
-    line_send(5, 0)
     line_take(4, 0)
     forward(0)
     line_take(4, 1)

time: 92.5 us -> 89 us (0.962)
  Pallas kernels: 90.5 us -> 86.9 us
    pallas_call x1, Pallas kernels: 90.5 us -> 86.9 us  [cube(): pl.pallas_call(kernel, out_shape=jax.ShapeDtypeStruct((tok_count, out_wid...]
where the time goes in v4:
time: 89 us; the launch traced here: 88.5 us
  Pallas kernels  86.9 us (98%)
  local copies, waits for them, and re-layouts  1.65 us (2%)
    pallas_call x1, Pallas kernels, cube(): pl.pallas_call(kernel, out_shape=jax.ShapeDtypeStruct((tok_count, out_wid...  86.9 us

profile of v4, /device:TPU:0, one launch (start us, length us, event | category | flops | bytes accessed | tf_op | source)
XLA Modules:
  0.0 88.5 jit_solution(8025120810991640517)
XLA Ops:
  0.0 86.9 %shard_map.91 = bf16[128,896]{1,0:T(8,128)(2,1)} custom-call(bf16[128,896]{1,0:T(8,128)(2,1)} %refs_0_.1, s32[4,128]{1,0:T(4,128)} %bitcast.8, f32[4,128]{1,0:T(4,128)} %bitcast.9, bf16[3584,512]{1,0:T(8,128)(2,1)} %bitcast.5, bf16[3584,512]{1,0:T(8,128)(2,1)} %bitcast.6, bf16[2048,896]{1,0:T(8,128)(2,1)} %bitcast.7, bf16[3584,512]{1,0:T(8,128)(2,1)} %refs_6_.1, ...), custom_call_target="tpu_custom_call" | custom-call | tf_op jit(solution)/shard_map/pallas_call | solution.py:536
  86.9 1.6 %copy.11 = bf16[128,896]{1,0:T(8,128)(2,1)} copy(bf16[128,896]{1,0:T(8,128)(2,1)} %shard_map.91) | data formatting | bytes 458752
